TPU v7x, 32 devices: a whole 2x2x4 slice. The times are simulated.
32 devices in a mesh: pert: 2 (over y), ga: 4 (over z), band: 4 (over x, core).
Axes of the slice: x: 2, y: 2, z: 4, core: 2. Of those that a mesh axis runs over, the one named last changes fastest.
Arguments:
- psi: float32 [2, 4, 131072], P(None, 'band', 'ga'), may hold values from -6 to 6
- potential: float32 [256, 128, 128], P('pert', 'ga'), parts along dimension 0, may hold values from 1 to 3
- miller: int32 [131072], replicated, may hold values from 0 to 2097151, as said below
- occupied: int32 [4], replicated, may hold values 0 or 1
Outputs:
- projected: float32 [2, 8, 131072], P(None, ('pert', 'band'), 'ga'), parts along dimension 1
There are 2 independent parts, one for each index of `pert`. A program takes and returns all parts, laid end to end along the dimension named above; an argument that names none is the same for every part. Nothing has to cross between parts.
Inputs may be any that keep to these rules, and one draw needn't show every extreme that they name: `miller`: entry k is the flat index a 128^2 + b * 128 + c of coefficient k, with Fourier indices a, b, c in 0..127 taken modulo 128; the entries are distinct; each of a, b, c, read as a signed index in -64..128/2-1, lies in -32..128/4-1; the j-th block of 32768 entries holds only points whose signed a plus 128/4 is congruent to j modulo 131072/32768.
All inputs are finite; a program needn't handle non-finite values.
Results may differ from a plain program's by a relative error of at most 0.00013.
Values sent between devices are 32-bit elements; how exact they have to be, the bound alone decides.
A program may use at most 64 MiB of HBM per device.

v0:
```python
import jax
import jax.numpy as jnp
from jax import lax
from jax.sharding import PartitionSpec as P

NPW = 131072
highest = lax.Precision.HIGHEST


def phases(first_index, second_index, direction, length):
    turns = first_index[:, None] * second_index[None, :] % length
    angle = direction * 2.0 * jnp.pi / length * turns.astype(jnp.float32)
    return (jnp.cos(angle), jnp.sin(angle))


def contract(pattern, real_part, imag_part, twiddle):
    cosine, sine_part = twiddle
    out_real = jnp.einsum(pattern, real_part, cosine, precision=highest) - jnp.einsum(
        pattern, imag_part, sine_part, precision=highest
    )
    out_imag = jnp.einsum(pattern, real_part, sine_part, precision=highest) + jnp.einsum(
        pattern, imag_part, cosine, precision=highest
    )
    return (out_real, out_imag)


def inner_products(left_real, left_imag, right_real, right_imag):
    over_real = jnp.einsum("mk,nk->mn", left_real, right_real, precision=highest) + jnp.einsum(
        "mk,nk->mn", left_imag, right_imag, precision=highest
    )
    over_imag = jnp.einsum("mk,nk->mn", left_real, right_imag, precision=highest) - jnp.einsum(
        "mk,nk->mn", left_imag, right_real, precision=highest
    )
    return (over_real, over_imag)


def subtract(applied_real, applied_imag, basis_real, basis_imag, weight_real, weight_imag):
    proj_real = jnp.einsum("mn,mk->nk", weight_real, basis_real, precision=highest) - jnp.einsum(
        "mn,mk->nk", weight_imag, basis_imag, precision=highest
    )
    proj_imag = jnp.einsum("mn,mk->nk", weight_imag, basis_real, precision=highest) + jnp.einsum(
        "mn,mk->nk", weight_real, basis_imag, precision=highest
    )
    return (applied_real - proj_real, applied_imag - proj_imag)


def shards(psi, potential, miller, occupied):
    grid_size = potential.shape[0]
    owners = lax.axis_size("ga")
    quarter = grid_size // 4
    per_shard = psi.shape[2]
    band_count = psi.shape[1]
    owner_index = lax.axis_index("ga")
    kept_rows = grid_size // 2
    kept_planes = grid_size // (2 * owners)
    full_index = jnp.arange(grid_size, dtype=jnp.int32)
    kept_index = (jnp.arange(kept_rows, dtype=jnp.int32) + grid_size - quarter) % grid_size
    inverse_rows = phases(kept_index, full_index, 1.0, grid_size)
    forward_rows = phases(full_index, kept_index, -1.0, grid_size)
    slot_index = jnp.arange(owners * kept_planes, dtype=jnp.int32)
    plane_index = (
        slot_index // kept_planes + owners * (slot_index % kept_planes) + grid_size - quarter
    ) % grid_size
    inverse_planes = phases(plane_index, full_index, 1.0, grid_size)
    forward_planes = phases(full_index, plane_index, -1.0, grid_size)
    local_points = lax.dynamic_slice_in_dim(miller, owner_index * per_shard, per_shard)
    index_a = local_points // (grid_size * grid_size)
    index_b = local_points // grid_size % grid_size
    index_c = local_points % grid_size
    plane_pos = (index_a + quarter) % grid_size
    position = (plane_pos // owners * kept_rows + (index_b + quarter) % grid_size) * kept_rows + (
        index_c + quarter
    ) % grid_size
    slab_size = kept_planes * kept_rows * kept_rows
    real_part = jnp.zeros((band_count, slab_size), jnp.float32).at[:, position].set(psi[0])
    imag_part = jnp.zeros((band_count, slab_size), jnp.float32).at[:, position].set(psi[1])
    real_part = real_part.reshape(band_count, kept_planes, kept_rows, kept_rows)
    imag_part = imag_part.reshape(band_count, kept_planes, kept_rows, kept_rows)
    real_part, imag_part = contract("ntbc,by->ntyc", real_part, imag_part, inverse_rows)
    pieces = (
        lax.all_to_all(real_part, "ga", split_axis=2, concat_axis=1, tiled=True),
        lax.all_to_all(imag_part, "ga", split_axis=2, concat_axis=1, tiled=True),
    )
    wide_real, wide_imag = contract("nsyc,cz->nsyz", pieces[0], pieces[1], inverse_rows)
    pieces = (wide_real, wide_imag)
    wave_real, wave_imag = contract("nsyz,sx->nxyz", pieces[0], pieces[1], inverse_planes)
    wave_real = wave_real * potential
    wave_imag = wave_imag * potential
    wide_real, wide_imag = contract("nxyz,xs->nsyz", wave_real, wave_imag, forward_planes)
    narrow = contract("nsyz,zc->nsyc", wide_real, wide_imag, forward_rows)
    real_part = lax.all_to_all(narrow[0], "ga", split_axis=1, concat_axis=2, tiled=True)
    imag_part = lax.all_to_all(narrow[1], "ga", split_axis=1, concat_axis=2, tiled=True)
    real_part, imag_part = contract("ntyc,yb->ntbc", real_part, imag_part, forward_rows)
    inverse_volume = 1.0 / grid_size**3
    applied_real = real_part.reshape(band_count, slab_size)[:, position] * inverse_volume
    applied_imag = imag_part.reshape(band_count, slab_size)[:, position] * inverse_volume
    weights = occupied.astype(jnp.float32)[:, None]
    moved_parts = (
        lax.all_to_all(applied_real, "band", split_axis=1, concat_axis=0, tiled=True),
        lax.all_to_all(applied_imag, "band", split_axis=1, concat_axis=0, tiled=True),
        lax.all_to_all(psi[0], "band", split_axis=1, concat_axis=0, tiled=True),
        lax.all_to_all(psi[1], "band", split_axis=1, concat_axis=0, tiled=True),
    )
    column_real, column_imag, basis_real, basis_imag = moved_parts
    over_real, over_imag = inner_products(basis_real, basis_imag, column_real, column_imag)
    over_real, over_imag = lax.psum((over_real, over_imag), ("ga", "band"))
    weight_real = weights * (over_real / NPW)
    weight_imag = weights * (over_imag / NPW)
    left_real, left_imag = subtract(
        column_real, column_imag, basis_real, basis_imag, weight_real, weight_imag
    )
    left_real, left_imag = (
        lax.all_to_all(left_real, "band", split_axis=0, concat_axis=1, tiled=True),
        lax.all_to_all(left_imag, "band", split_axis=0, concat_axis=1, tiled=True),
    )
    return jnp.stack([left_real, left_imag])


def solution(mesh):
    in_specs = (P(None, "band", "ga"), P("pert", "ga", None), P(), P())
    out_specs = P(None, ("pert", "band"), "ga")
    return jax.shard_map(shards, mesh=mesh, in_specs=in_specs, out_specs=out_specs, check_vma=False)
```

profile of v0, /device:TPU:0, one launch (start us, length us, event | category | flops | bytes accessed | tf_op | source)
XLA Modules:
  0.0 796.2 jit_solution(8780782208961339326)
XLA Ops:
  3.1 120.4 %scatter_custom_fusion.1 = f32[65536]{0:T(1024)S(1)} fusion(s32[32768]{0:T(1024)S(1)} %get-tuple-element.8, f32[32768]{0:T(1024)} %bitcast.7, f32[]{:T(128)} %constant.167.clone.1), kind=kCustom, calls=%fused_computation.97 | custom fusion | bytes 262656 | tf_op jit(solution)/shard_map/scatter | solution.py:76
  123.8 120.4 %scatter_custom_fusion = f32[65536]{0:T(1024)S(1)} fusion(s32[32768]{0:T(1024)S(1)} %get-tuple-element.8, f32[32768]{0:T(1024)} %bitcast.3, f32[]{:T(128)} %constant.167.clone.1), kind=kCustom, calls=%fused_computation.99 | custom fusion | bytes 262656 | tf_op jit(solution)/shard_map/scatter | solution.py:75
  248.2 6.3 all-to-all-start
  258.1 10.9 %all-to-all-done = f32[4,1,32768]{2,1,0:T(1,128)S(1)} async-done(((f32[4,1,32768]{2,1,0:T(1,128)}), f32[4,1,32768]{2,1,0:T(1,128)S(1)}, u32[]{:S(2)}, u32[]{:S(2)}) %all-to-all-start) | async-done | bytes 524320 | tf_op jit(solution)/shard_map/all_to_all | solution.py:81
  269.0 3.6 all-to-all-start.1
  278.8 7.7 all-to-all-done.1
  299.5 3.6 subtract_multiply_fusion
  306.0 3.6 add_multiply_fusion
  318.0 3.5 all-to-all-start.2
  326.5 9.0 %all-to-all-done.2 = f32[4,1,32768]{2,1,0:T(1,128)S(1)} async-done(((f32[4,1,32768]{2,1,0:T(1,128)}), f32[4,1,32768]{2,1,0:T(1,128)S(1)}, u32[]{:S(2)}, u32[]{:S(2)}) %all-to-all-start.2) | async-done | bytes 524320 | tf_op jit(solution)/shard_map/all_to_all | solution.py:91
  335.5 3.6 all-to-all-start.3
  343.7 9.4 %all-to-all-done.3 = f32[4,1,32768]{2,1,0:T(1,128)S(1)} async-done(((f32[4,1,32768]{2,1,0:T(1,128)}), f32[4,1,32768]{2,1,0:T(1,128)S(1)}, u32[]{:S(2)}, u32[]{:S(2)}) %all-to-all-start.3) | async-done | bytes 524320 | tf_op jit(solution)/shard_map/all_to_all | solution.py:92
  353.1 3.3 all-to-all-start.5
  360.3 180.5 %gather_fusion = f32[32768]{0:T(1024)S(1)} fusion(f32[65536]{0:T(1024)S(1)} %reshape.289, s32[32768]{0:T(1024)S(1)} %get-tuple-element.7), kind=kCustom, calls=%fused_computation | custom fusion | bytes 393216 | tf_op jit(solution)/shard_map/gather | solution.py:95
  542.5 180.5 %gather_fusion.1 = f32[32768]{0:T(1024)S(1)} fusion(f32[65536]{0:T(1024)S(1)} %reshape.299, s32[32768]{0:T(1024)S(1)} %get-tuple-element.7), kind=kCustom, calls=%fused_computation.1 | custom fusion | bytes 393216 | tf_op jit(solution)/shard_map/gather | solution.py:96
  723.1 3.3 all-to-all-start.4
  727.1 3.9 all-to-all-done.4
  735.0 3.9 all-to-all-done.6
  738.9 3.3 all-to-all-start.7
  742.9 3.9 all-to-all-done.7
  748.2 30.3 %all-reduce = (f32[4,4]{0,1:T(4,128)S(1)}, f32[4,4]{0,1:T(4,128)S(1)}) all-reduce(f32[4,4]{0,1:T(4,128)S(1)} %fusion.8, f32[4,4]{0,1:T(4,128)S(1)} %fusion.9), channel_id=1, replica_groups=mesh['pert'=2,'ga'=4,'band'=4] {'ga','band'}, use_global_device_ids=true, to_apply=%region_3.4 | all-reduce | flops 32 | bytes 256 | tf_op jit(solution)/shard_map/psum | solution.py:106
  780.2 3.3 all-to-all-start.8
  784.5 3.5 all-to-all-done.8
  788.1 7.0 all_to_all.144
  (75 shorter events, 66.5 us)
Async XLA Ops:
  248.2 20.8 %all-to-all-start = ((f32[4,1,32768]{2,1,0:T(1,128)}), f32[4,1,32768]{2,1,0:T(1,128)S(1)}, u32[]{:S(2)}, u32[]{:S(2)}) async-start(f32[4,1,32768]{2,1,0:T(1,128)} %reshape.365), calls=%async_computation | async-start | bytes 1048576 | tf_op jit(solution)/shard_map/all_to_all | solution.py:81
  269.0 17.5 %all-to-all-start.1 = ((f32[4,1,32768]{2,1,0:T(1,128)}), f32[4,1,32768]{2,1,0:T(1,128)S(1)}, u32[]{:S(2)}, u32[]{:S(2)}) async-start(f32[4,1,32768]{2,1,0:T(1,128)} %reshape.367), calls=%async_computation.1 | async-start | bytes 1048576 | tf_op jit(solution)/shard_map/all_to_all | solution.py:82
  297.9 1.6 copy-start
  318.0 17.5 %all-to-all-start.2 = ((f32[4,1,32768]{2,1,0:T(1,128)}), f32[4,1,32768]{2,1,0:T(1,128)S(1)}, u32[]{:S(2)}, u32[]{:S(2)}) async-start(f32[4,1,32768]{2,1,0:T(1,128)} %reshape.369), calls=%async_computation.2 | async-start | bytes 1048576 | tf_op jit(solution)/shard_map/all_to_all | solution.py:91
  335.5 17.6 %all-to-all-start.3 = ((f32[4,1,32768]{2,1,0:T(1,128)}), f32[4,1,32768]{2,1,0:T(1,128)S(1)}, u32[]{:S(2)}, u32[]{:S(2)}) async-start(f32[4,1,32768]{2,1,0:T(1,128)} %reshape.371), calls=%async_computation.3 | async-start | bytes 1048576 | tf_op jit(solution)/shard_map/all_to_all | solution.py:92
  353.1 370.0 %all-to-all-start.5 = ((f32[1,4,8192]{2,0,1:T(1,128)}), f32[1,4,8192]{2,0,1:T(1,128)S(1)}, u32[]{:S(2)}, u32[]{:S(2)}) async-start(f32[1,4,8192]{2,0,1:T(1,128)} %bitcast.45), calls=%async_computation.5 | async-start | bytes 262144 | tf_op jit(solution)/shard_map/all_to_all | solution.py:101
  723.0 25.2 %copy-start.1 = (s32[4]{0:T(128)S(1)}, s32[4]{0:T(128)}, u32[]{:S(2)}) copy-start(s32[4]{0:T(128)} %param.7) | copy-start | bytes 52
  723.1 7.9 all-to-all-start.4
  731.0 7.9 all-to-all-start.6
  738.9 7.9 all-to-all-start.7
  780.2 7.9 all-to-all-start.8
where the time goes:
time: 803 us; the launch traced here: 796 us
  local copies, waits for them, and re-layouts  617 us (77%)
  waiting for transfers between devices  52.2 us (7%)
  matrix products  41.5 us (5%)
  blocking collectives  37.2 us (5%)
  starting transfers between devices  33.7 us (4%)
  other arithmetic  13.3 us (2%)
    gather x1, local copies, waits for them, and re-layouts, shards(): real_part.reshape(band_count, slab_size)[:, position] * inverse_volume  181 us
    gather x1, local copies, waits for them, and re-layouts, shards(): imag_part.reshape(band_count, slab_size)[:, position] * inverse_volume  181 us
    scatter x1, local copies, waits for them, and re-layouts, shards(): jnp.zeros((band_count, slab_size), jnp.float32).at[:, position].set(psi[0])  120 us
    scatter x1, local copies, waits for them, and re-layouts, shards(): jnp.zeros((band_count, slab_size), jnp.float32).at[:, position].set(psi[1])  120 us
    psum x1, blocking collectives, shards(): over_real, over_imag = lax.psum((over_real, over_imag), ('ga', 'band'))  30.3 us
  transfers between devices with their start and end apart: 9, of which 8 were waited for; matrix products, arithmetic and copies ran while one was open for 49% of the time, Pallas kernels for 0%

commit v1 on v0

--- a/solution.py
+++ b/solution.py
@@ -78,7 +78,12 @@
     imag_part = imag_part.reshape(band_count, kept_planes, kept_rows, kept_rows)
     real_part, imag_part = contract("ntbc,by->ntyc", real_part, imag_part, inverse_rows)
     pieces = (
-        lax.all_to_all(real_part, "ga", split_axis=2, concat_axis=1, tiled=True),
+        jnp.concatenate(
+            lax.all_to_all(
+                jnp.stack(jnp.split(real_part, lax.axis_size("ga"), axis=2)), "ga", 0, 0
+            ),
+            axis=1,
+        ),
         lax.all_to_all(imag_part, "ga", split_axis=2, concat_axis=1, tiled=True),
     )
     wide_real, wide_imag = contract("nsyc,cz->nsyz", pieces[0], pieces[1], inverse_rows)

time: 803 us -> 808 us (level)
  transfers between devices with their start and end apart: 9 -> 9, of which waited for: 8 -> 8; matrix products, arithmetic and copies ran while one was open for 49% -> 48% of each run, Pallas kernels for 0% -> 0%
where the time goes in v1:
time: 808 us; the launch traced here: 801 us
  local copies, waits for them, and re-layouts  620 us (77%)
  waiting for transfers between devices  52.9 us (7%)
  matrix products  41.5 us (5%)
  blocking collectives  37.2 us (5%)
  starting transfers between devices  34.4 us (4%)
  other arithmetic  14.2 us (2%)
    gather x1, local copies, waits for them, and re-layouts, shards(): imag_part.reshape(band_count, slab_size)[:, position] * inverse_volume  181 us
    gather x1, local copies, waits for them, and re-layouts, shards(): real_part.reshape(band_count, slab_size)[:, position] * inverse_volume  181 us
    scatter x1, local copies, waits for them, and re-layouts, shards(): jnp.zeros((band_count, slab_size), jnp.float32).at[:, position].set(psi[0])  120 us
    scatter x1, local copies, waits for them, and re-layouts, shards(): jnp.zeros((band_count, slab_size), jnp.float32).at[:, position].set(psi[1])  120 us
    psum x1, blocking collectives, shards(): over_real, over_imag = lax.psum((over_real, over_imag), ('ga', 'band'))  30.3 us
  transfers between devices with their start and end apart: 9, of which 8 were waited for; matrix products, arithmetic and copies ran while one was open for 48% of the time, Pallas kernels for 0%

profile of v1, /device:TPU:0, one launch (start us, length us, event | category | flops | bytes accessed | tf_op | source)
XLA Modules:
  0.0 800.8 jit_solution(4541529143578964517)
XLA Ops:
  3.1 120.4 %scatter_custom_fusion.1 = f32[65536]{0:T(1024)S(1)} fusion(s32[32768]{0:T(1024)S(1)} %get-tuple-element.8, f32[32768]{0:T(1024)} %bitcast.7, f32[]{:T(128)} %constant.167.clone.1), kind=kCustom, calls=%fused_computation.102 | custom fusion | bytes 262656 | tf_op jit(solution)/shard_map/scatter | solution.py:76
  123.8 120.4 %scatter_custom_fusion = f32[65536]{0:T(1024)S(1)} fusion(s32[32768]{0:T(1024)S(1)} %get-tuple-element.8, f32[32768]{0:T(1024)} %bitcast.3, f32[]{:T(128)} %constant.167.clone.1), kind=kCustom, calls=%fused_computation.104 | custom fusion | bytes 262656 | tf_op jit(solution)/shard_map/scatter | solution.py:75
  251.2 6.4 all-to-all-start
  261.1 10.9 %all-to-all-done = f32[4,1,32768]{2,1,0:T(1,128)S(1)} async-done(((f32[4,1,32768]{2,1,0:T(1,128)}), f32[4,1,32768]{2,1,0:T(1,128)S(1)}, u32[]{:S(2)}, u32[]{:S(2)}) %all-to-all-start) | async-done | bytes 524320 | tf_op jit(solution)/shard_map/all_to_all | solution.py:82
  272.1 4.3 all-to-all-start.1
  282.0 8.4 %all-to-all-done.1 = f32[4,1,32768]{2,1,0:T(1,128)} async-done(((f32[4,1,32768]{2,1,0:T(1,128)}), f32[4,1,32768]{2,1,0:T(1,128)}, u32[]{:S(2)}, u32[]{:S(2)}) %all-to-all-start.1) | async-done | bytes 524320 | tf_op jit(solution)/shard_map/all_to_all | solution.py:87
  290.3 3.8 reduce.1
  304.2 3.6 subtract_multiply_fusion
  310.7 3.6 add_multiply_fusion
  322.6 3.5 all-to-all-start.2
  331.1 9.0 %all-to-all-done.2 = f32[4,1,32768]{2,1,0:T(1,128)S(1)} async-done(((f32[4,1,32768]{2,1,0:T(1,128)}), f32[4,1,32768]{2,1,0:T(1,128)S(1)}, u32[]{:S(2)}, u32[]{:S(2)}) %all-to-all-start.2) | async-done | bytes 524320 | tf_op jit(solution)/shard_map/all_to_all | solution.py:96
  340.1 3.6 all-to-all-start.3
  348.2 9.5 %all-to-all-done.3 = f32[4,1,32768]{2,1,0:T(1,128)S(1)} async-done(((f32[4,1,32768]{2,1,0:T(1,128)}), f32[4,1,32768]{2,1,0:T(1,128)S(1)}, u32[]{:S(2)}, u32[]{:S(2)}) %all-to-all-start.3) | async-done | bytes 524320 | tf_op jit(solution)/shard_map/all_to_all | solution.py:97
  364.8 180.5 %gather_fusion = f32[32768]{0:T(1024)S(1)} fusion(f32[65536]{0:T(1024)S(1)} %reshape.290, s32[32768]{0:T(1024)S(1)} %get-tuple-element.7), kind=kCustom, calls=%fused_computation | custom fusion | bytes 393216 | tf_op jit(solution)/shard_map/gather | solution.py:100
  547.1 180.5 %gather_fusion.1 = f32[32768]{0:T(1024)S(1)} fusion(f32[65536]{0:T(1024)S(1)} %reshape.300, s32[32768]{0:T(1024)S(1)} %get-tuple-element.7), kind=kCustom, calls=%fused_computation.1 | custom fusion | bytes 393216 | tf_op jit(solution)/shard_map/gather | solution.py:101
  727.6 3.3 all-to-all-start.4
  731.6 3.9 all-to-all-done.4
  739.6 3.9 all-to-all-done.6
  743.4 3.3 all-to-all-start.7
  747.5 3.9 all-to-all-done.7
  752.8 30.3 %all-reduce = (f32[4,4]{0,1:T(4,128)S(1)}, f32[4,4]{0,1:T(4,128)S(1)}) all-reduce(f32[4,4]{0,1:T(4,128)S(1)} %fusion.8, f32[4,4]{0,1:T(4,128)S(1)} %fusion.9), channel_id=1, replica_groups=mesh['pert'=2,'ga'=4,'band'=4] {'ga','band'}, use_global_device_ids=true, to_apply=%region_3.4 | all-reduce | flops 32 | bytes 256 | tf_op jit(solution)/shard_map/psum | solution.py:111
  784.8 3.3 all-to-all-start.8
  789.1 3.5 all-to-all-done.8
  792.7 7.0 all_to_all.134
  (75 shorter events, 69.2 us)
Async XLA Ops:
  251.2 20.8 %all-to-all-start = ((f32[4,1,32768]{2,1,0:T(1,128)}), f32[4,1,32768]{2,1,0:T(1,128)S(1)}, u32[]{:S(2)}, u32[]{:S(2)}) async-start(f32[4,1,32768]{2,1,0:T(1,128)} %reshape.366), calls=%async_computation | async-start | bytes 1048576 | tf_op jit(solution)/shard_map/all_to_all | solution.py:82
  272.1 18.3 %all-to-all-start.1 = ((f32[4,1,32768]{2,1,0:T(1,128)}), f32[4,1,32768]{2,1,0:T(1,128)}, u32[]{:S(2)}, u32[]{:S(2)}) async-start(f32[4,1,32768]{2,1,0:T(1,128)} %reshape.368), calls=%async_computation.1 | async-start | bytes 1048576 | tf_op jit(solution)/shard_map/all_to_all | solution.py:87
  302.6 1.6 copy-start
  322.6 17.5 %all-to-all-start.2 = ((f32[4,1,32768]{2,1,0:T(1,128)}), f32[4,1,32768]{2,1,0:T(1,128)S(1)}, u32[]{:S(2)}, u32[]{:S(2)}) async-start(f32[4,1,32768]{2,1,0:T(1,128)} %reshape.370), calls=%async_computation.2 | async-start | bytes 1048576 | tf_op jit(solution)/shard_map/all_to_all | solution.py:96
  340.1 17.6 %all-to-all-start.3 = ((f32[4,1,32768]{2,1,0:T(1,128)}), f32[4,1,32768]{2,1,0:T(1,128)S(1)}, u32[]{:S(2)}, u32[]{:S(2)}) async-start(f32[4,1,32768]{2,1,0:T(1,128)} %reshape.372), calls=%async_computation.3 | async-start | bytes 1048576 | tf_op jit(solution)/shard_map/all_to_all | solution.py:97
  357.7 369.9 %all-to-all-start.5 = ((f32[1,4,8192]{2,0,1:T(1,128)}), f32[1,4,8192]{2,0,1:T(1,128)S(1)}, u32[]{:S(2)}, u32[]{:S(2)}) async-start(f32[1,4,8192]{2,0,1:T(1,128)} %bitcast.48), calls=%async_computation.5 | async-start | bytes 262144 | tf_op jit(solution)/shard_map/all_to_all | solution.py:106
  727.6 25.2 %copy-start.1 = (s32[4]{0:T(128)S(1)}, s32[4]{0:T(128)}, u32[]{:S(2)}) copy-start(s32[4]{0:T(128)} %param.7) | copy-start | bytes 52
  727.6 7.9 all-to-all-start.4
  735.5 7.9 all-to-all-start.6
  743.4 7.9 all-to-all-start.7
  784.8 7.9 all-to-all-start.8
